TPU v7x, 512 devices: a whole 4x8x8 slice. The times are simulated.
512 devices in a mesh: seq: 64 (over y, z_lo, core), tensor: 8 (over z_hi, x).
Axes of the slice: x: 4, y: 8, z: 8 (z_hi: 2, z_lo: 4; z = z_hi * 4 + z_lo), core: 2. Of those that a mesh axis runs over, the one named last changes fastest.
Arguments:
- queries: bfloat16 [16384, 3072], P('seq', 'tensor'), may hold values from -100 to 100
- key_tiles: bfloat16 [16384, 3072], P('seq', 'tensor'), may hold values from -6 to 6
- value_tiles: bfloat16 [16384, 3072], P('seq', 'tensor'), may hold values from -6 to 6
- cache_keys: bfloat16 [128, 128, 3072], P('seq', None, 'tensor'), may hold values from -6 to 6
- cache_values: bfloat16 [128, 128, 3072], P('seq', None, 'tensor'), may hold values from -6 to 6
- hidden: bfloat16 [16384, 5120], P('seq', 'tensor'), may hold values from -6 to 6
- out_weight: bfloat16 [3072, 5120], P('seq', 'tensor'), may hold values from -0.21875 to 0.21875
- gate_table: float32 [1000, 5120], P(None, 'tensor'), may hold values from 0.3 to 2.5
- lengths: int32 [16], replicated, may hold values from 512 to 1536, as said below
- page_table: int32 [16, 4], replicated, may hold values from 0 to 127, as said below
- page_count: int32 [16], replicated, may hold values from 0 to 4
- timestep: int32 [16], replicated, may hold values from 0 to 999
Outputs:
- layer_out: bfloat16 [16384, 5120], P('seq', 'tensor')
Inputs may be any that keep to these rules, and one draw needn't show every extreme that they name: The lengths sum to 16384. `page_table`: a page named by clip c lies on a seq index that holds some token of clip c (page p lies on seq index p // 2); a page may be named by several clips or twice.
All inputs are finite; a program needn't handle non-finite values.
Results may differ from a plain program's by a relative error of at most 0.018.
Values may be sent and summed in bfloat16 or wider, within the bound.
No kernel may reach another device: no remote copies, remote signals or barrier semaphores. Data moves between devices by JAX's collectives and lax.ppermute only.
A program may use at most 64 MiB of HBM per device.

v0:
```python
import math
import jax
import jax.numpy as jnp
from jax import lax
from jax.sharding import PartitionSpec as P

HD = 128
PAGE = 128
POOL = 2
REACH = 6
low_score = -1e30


def shifted(block, axis, distance):
    devices = range(lax.axis_size(axis))
    route = [(i - distance, i) for i in devices if i - distance in devices]
    return lax.ppermute(block, axis, route)


def clip_index(positions, clip_ends):
    return jnp.sum((positions[:, None] >= clip_ends[None, :]).astype(jnp.int32), axis=1)


def allowed_keys(query_clip, source, clip_ends, page_table, page_count, block_total, row_count):
    key_pos = source * row_count + jnp.arange(row_count, dtype=jnp.int32)
    in_range = (source >= 0) & (source < block_total)
    same_clip = (query_clip[:, None] == clip_index(key_pos, clip_ends)[None, :]) & in_range
    clip_total = clip_ends.shape[0]
    page_ids = source * POOL + jnp.arange(POOL, dtype=jnp.int32)
    live_slots = jnp.arange(page_table.shape[1], dtype=jnp.int32)[None, :] < page_count[:, None]
    named_pages = jnp.any(
        live_slots[:, :, None] & (page_table[:, :, None] == page_ids[None, None, :]), axis=1
    )
    member = query_clip[:, None] == jnp.arange(clip_total, dtype=jnp.int32)[None, :]
    page_ok = jnp.any(member[:, :, None] & named_pages[None], axis=1) & in_range
    page_ok = jnp.repeat(page_ok, PAGE, axis=1)
    return jnp.concatenate([same_clip, page_ok], axis=1)


def attend(carry_state, query_heads, key_heads, value_heads, allowed):
    running_max, totals, accumulated = carry_state
    scores = jnp.einsum(
        "qhd,khd->hqk", query_heads, key_heads, preferred_element_type=jnp.float32
    ) * (1.0 / math.sqrt(HD))
    scores = jnp.where(allowed[None], scores, low_score)
    new_max = jnp.maximum(running_max, jnp.max(scores, axis=2))
    factor = jnp.exp(running_max - new_max)
    weights = jnp.where(allowed[None], jnp.exp(scores - new_max[:, :, None]), 0.0)
    totals = totals * factor + jnp.sum(weights, axis=2)
    accumulated = accumulated * factor[:, :, None] + jnp.einsum(
        "hqk,khd->hqd",
        weights.astype(jnp.bfloat16),
        value_heads,
        preferred_element_type=jnp.float32,
    )
    return (new_max, totals, accumulated)


def empty_state(head_count, row_count):
    return (
        jnp.full((head_count, row_count), low_score, jnp.float32),
        jnp.zeros((head_count, row_count), jnp.float32),
        jnp.zeros((head_count, row_count, HD), jnp.float32),
    )


def visit_block(carry_state, packed, source, query_heads, query_clip, context):
    clip_ends, page_table, page_count, block_total = context
    row_count = query_heads.shape[0]
    head_count = query_heads.shape[1]
    allowed = allowed_keys(
        query_clip, source, clip_ends, page_table, page_count, block_total, row_count
    )
    key_heads = packed[0].reshape(-1, head_count, HD)
    value_heads = packed[1].reshape(-1, head_count, HD)
    return attend(carry_state, query_heads, key_heads, value_heads, allowed)


def fetch_direct(packed, offset):
    return shifted(packed, "seq", offset)


def local(
    queries,
    key_tiles,
    value_tiles,
    cache_keys,
    cache_values,
    hidden,
    out_weight,
    gate_table,
    lengths,
    page_table,
    page_count,
    timestep,
):
    row_count = queries.shape[0]
    tile_width = queries.shape[1]
    head_count = tile_width // HD
    block_total = lax.axis_size("seq")
    seq_index = lax.axis_index("seq")
    clip_ends = jnp.cumsum(lengths, dtype=jnp.int32)
    row_ids = jnp.arange(row_count, dtype=jnp.int32)
    positions = seq_index * row_count + row_ids
    query_clip = clip_index(positions, clip_ends)
    query_heads = queries.reshape(row_count, head_count, HD)
    context = (clip_ends, page_table, page_count, block_total)
    packed = jnp.stack(
        [
            jnp.concatenate([key_tiles, cache_keys.reshape(-1, tile_width)], axis=0),
            jnp.concatenate([value_tiles, cache_values.reshape(-1, tile_width)], axis=0),
        ]
    )
    carry_state = visit_block(
        empty_state(head_count, row_count), packed, seq_index, query_heads, query_clip, context
    )
    for offset in range(1, REACH + 1):
        from_below = fetch_direct(packed, offset)
        carry_state = visit_block(
            carry_state, from_below, seq_index - offset, query_heads, query_clip, context
        )
        from_above = fetch_direct(packed, -offset)
        carry_state = visit_block(
            carry_state, from_above, seq_index + offset, query_heads, query_clip, context
        )
    running_max, totals, accumulated = carry_state
    result = accumulated / totals[:, :, None]
    attention_local = (
        jnp.transpose(result, (1, 0, 2)).reshape(row_count, tile_width).astype(jnp.bfloat16)
    )
    attention = lax.all_gather(attention_local, "tensor", axis=1, tiled=True)
    projected = jnp.dot(
        attention,
        lax.all_gather(out_weight, "seq", axis=0, tiled=True),
        preferred_element_type=jnp.float32,
    )
    clip_total = lengths.shape[0]
    step_onehot = (
        timestep[:, None] == jnp.arange(gate_table.shape[0], dtype=jnp.int32)[None, :]
    ).astype(jnp.float32)
    clip_gate = jnp.dot(
        step_onehot, gate_table, precision=lax.Precision.HIGHEST, preferred_element_type=jnp.float32
    )
    clip_onehot = (query_clip[:, None] == jnp.arange(clip_total, dtype=jnp.int32)[None, :]).astype(
        jnp.float32
    )
    token_gate = jnp.dot(
        clip_onehot, clip_gate, precision=lax.Precision.HIGHEST, preferred_element_type=jnp.float32
    )
    return (hidden.astype(jnp.float32) + token_gate * projected).astype(jnp.bfloat16)


def solution(mesh):
    return jax.shard_map(
        local,
        mesh=mesh,
        in_specs=(
            P("seq", "tensor"),
            P("seq", "tensor"),
            P("seq", "tensor"),
            P("seq", None, "tensor"),
            P("seq", None, "tensor"),
            P("seq", "tensor"),
            P("seq", "tensor"),
            P(None, "tensor"),
            P(),
            P(),
            P(),
            P(),
        ),
        out_specs=P("seq", "tensor"),
        check_vma=False,
    )
```

profile of v0, /device:TPU:1, one launch (start us, length us, event | category | flops | bytes accessed | tf_op | source)
XLA Modules:
  0.0 506.3 jit_solution(10120251715169249315)
XLA Ops:
  6.5 1.2 copy.107
  7.8 1.1 copy.113
  8.8 1.1 copy.196
  10.0 1.1 copy.197
  11.1 1.0 pad_maximum_fusion
  12.1 1.3 collective-permute-start.9
  13.4 10.5 %collective-permute-start.8 = (bf16[2,512,384]{1,2,0:T(8,128)(2,1)}, bf16[2,512,384]{1,2,0:T(8,128)(2,1)}, u32[]{:S(2)}, u32[]{:S(2)}) collective-permute-start(bf16[2,512,384]{1,2,0:T(8,128)(2,1)} %pad_maximum_fusion), channel_id=1, source_target_pairs={{0,40},{8,48},{16,56},{24,64},{32,72},{40,80},{48,88},{56,96},{64,... | collective-permute-start | bytes 2359304 | tf_op jit(solution)/shard_map/ppermute | solution.py:17
  23.9 1.3 collective-permute-start.7
  25.2 5.8 %collective-permute-start.6 = (bf16[2,512,384]{1,2,0:T(8,128)(2,1)}, bf16[2,512,384]{1,2,0:T(8,128)(2,1)}, u32[]{:S(2)}, u32[]{:S(2)}) collective-permute-start(bf16[2,512,384]{1,2,0:T(8,128)(2,1)} %pad_maximum_fusion), channel_id=1, source_target_pairs={{0,32},{8,40},{16,48},{24,56},{32,64},{40,72},{48,80},{56,88},{64,... | collective-permute-start | bytes 2359304 | tf_op jit(solution)/shard_map/ppermute | solution.py:17
  31.0 1.3 collective-permute-start.5
  32.8 0.7 convert_reduce_fusion
  33.5 1.1 copy.111
  34.6 0.8 copy.109
  35.4 0.7 copy.110
  36.3 0.7 and_reduce_fusion
  37.2 0.6 compare_and_fusion.10
  38.1 0.7 pad_add_fusion.4
  38.8 0.7 pad_add_fusion.3
  39.5 0.7 pad_add_fusion.2
  40.1 0.7 broadcast_and_fusion.12
  40.8 0.9 compare_and_fusion.1
  41.8 2.6 fusion.175
  44.5 0.7 pad_add_fusion.11
  45.2 0.7 pad_add_fusion.1
  45.9 0.7 pad_add_fusion.12
  46.5 1.8 copy.114
  48.3 1.7 concatenate.64
  50.0 5.2 %collective-permute-start.4 = (bf16[2,512,384]{1,2,0:T(8,128)(2,1)}, bf16[2,512,384]{1,2,0:T(8,128)(2,1)S(1)}, u32[]{:S(2)}, u32[]{:S(2)}) collective-permute-start(bf16[2,512,384]{1,2,0:T(8,128)(2,1)} %pad_maximum_fusion), channel_id=1, source_target_pairs={{0,24},{8,32},{16,40},{24,48},{32,56},{40,64},{48,72},{56,80},{64,... | collective-permute-start | bytes 2359304 | tf_op jit(solution)/shard_map/ppermute | solution.py:17
  55.2 1.2 fusion.153
  56.4 64.8 %collective-permute-done.8 = bf16[2,512,384]{1,2,0:T(8,128)(2,1)} collective-permute-done((bf16[2,512,384]{1,2,0:T(8,128)(2,1)}, bf16[2,512,384]{1,2,0:T(8,128)(2,1)}, u32[]{:S(2)}, u32[]{:S(2)}) %collective-permute-start.8) | collective-permute-done | bytes 786464 | tf_op jit(solution)/shard_map/ppermute | solution.py:17
  121.2 1.3 collective-permute-start.3
  122.5 1.2 fusion.154
  123.7 4.0 collective-permute-start.2
  127.7 1.2 fusion.155
  128.9 9.2 %collective-permute-done.6 = bf16[2,512,384]{1,2,0:T(8,128)(2,1)} collective-permute-done((bf16[2,512,384]{1,2,0:T(8,128)(2,1)}, bf16[2,512,384]{1,2,0:T(8,128)(2,1)}, u32[]{:S(2)}, u32[]{:S(2)}) %collective-permute-start.6) | collective-permute-done | bytes 786464 | tf_op jit(solution)/shard_map/ppermute | solution.py:17
  138.0 43.7 %collective-permute-start.1 = (bf16[2,512,384]{1,2,0:T(8,128)(2,1)}, bf16[2,512,384]{1,2,0:T(8,128)(2,1)S(1)}, u32[]{:S(2)}, u32[]{:S(2)}) collective-permute-start(bf16[2,512,384]{1,2,0:T(8,128)(2,1)} %pad_maximum_fusion), channel_id=1, source_target_pairs={{8,0},{16,8},{24,16},{32,24},{40,32},{48,40},{56,48},{64,56},{72,6... | collective-permute-start | bytes 2359304 | tf_op jit(solution)/shard_map/ppermute | solution.py:17
  181.7 1.2 fusion.156
  182.9 23.6 %collective-permute-start.10 = (bf16[2,512,384]{1,2,0:T(8,128)(2,1)}, bf16[2,512,384]{1,2,0:T(8,128)(2,1)S(1)}, u32[]{:S(2)}, u32[]{:S(2)}) collective-permute-start(bf16[2,512,384]{1,2,0:T(8,128)(2,1)} %pad_maximum_fusion), channel_id=1, source_target_pairs={{0,48},{8,56},{16,64},{24,72},{32,80},{40,88},{48,96},{56,104},{64... | collective-permute-start | bytes 2359304 | tf_op jit(solution)/shard_map/ppermute | solution.py:17
  206.5 1.2 fusion.157
  207.7 34.8 %collective-permute-start = (bf16[2,512,384]{1,2,0:T(8,128)(2,1)}, bf16[2,512,384]{1,2,0:T(8,128)(2,1)S(1)}, u32[]{:S(2)}, u32[]{:S(2)}) collective-permute-start(bf16[2,512,384]{1,2,0:T(8,128)(2,1)} %pad_maximum_fusion), channel_id=1, source_target_pairs={{0,8},{8,16},{16,24},{24,32},{32,40},{40,48},{48,56},{56,64},{64,7... | collective-permute-start | bytes 2359304 | tf_op jit(solution)/shard_map/ppermute | solution.py:17
  242.6 0.5 fusion.165
  243.1 1.5 collective-permute-start.11
  244.6 0.5 fusion.166
  245.1 0.5 fusion.167
  245.7 0.5 fusion.168
  246.2 0.5 fusion.169
  246.7 0.5 fusion.170
  247.6 0.5 fusion.171
  248.5 0.5 fusion.172
  249.0 0.5 fusion.173
  249.5 19.1 %collective-permute-done = bf16[2,512,384]{1,2,0:T(8,128)(2,1)S(1)} collective-permute-done((bf16[2,512,384]{1,2,0:T(8,128)(2,1)}, bf16[2,512,384]{1,2,0:T(8,128)(2,1)S(1)}, u32[]{:S(2)}, u32[]{:S(2)}) %collective-permute-start) | collective-permute-done | bytes 786464 | tf_op jit(solution)/shard_map/ppermute | solution.py:17
  268.7 0.5 fusion.164
  269.2 0.5 fusion.174
  270.1 0.5 fusion.163
  270.6 0.5 copy-done.6
  276.6 0.5 fusion.43
  278.4 0.7 fusion.47
  281.4 1.1 fusion.54
  282.6 0.7 all-gather.5.cloned.1.call-update
  283.3 0.9 fusion.113
  284.3 0.5 fusion.146
  284.8 89.4 %all-gather.3.cloned.1.call-done = bf16[256,3072]{0,1:T(8,128)(2,1)} async-done(((bf16[256,384]{0,1:T(8,128)(2,1)}), bf16[256,3072]{0,1:T(8,128)(2,1)}) %all-gather.3.cloned.1.call-update) | async-done | bytes 1572880 | tf_op jit(solution)/shard_map/all_gather | solution.py:131
  374.2 120.5 %all-gather.5.cloned.1.call-done = bf16[3072,640]{1,0:T(8,128)(2,1)} async-done(((bf16[48,640]{1,0:T(8,128)(2,1)}), bf16[3072,640]{1,0:T(8,128)(2,1)}) %all-gather.5.cloned.1.call-update) | async-done | bytes 3932176 | tf_op jit(solution)/shard_map/all_gather | solution.py:134
  494.7 4.7 fusion.27
  (140 shorter events, 11.6 us)
Async XLA Ops:
  6.5 276.8 %copy-start = (f32[1000,640]{1,0:T(8,128)S(1)}, f32[1000,640]{1,0:T(8,128)}, u32[]{:S(2)}) copy-start(f32[1000,640]{1,0:T(8,128)} %param.19) | copy-start | bytes 7680004
  6.5 367.7 %all-gather.3.cloned.1.call-start = ((), (), s32[]{:S(2)}) async-start(), calls=%async_computation | async-start | bytes 1769472 | tf_op jit(solution)/shard_map/all_gather | solution.py:131
  8.8 3.3 copy-start.9
  11.0 21.4 %copy-start.8 = (bf16[2,128,384]{2,1,0:T(8,128)(2,1)S(1)}, bf16[2,128,384]{2,1,0:T(8,128)(2,1)}, u32[]{:S(2)}) copy-start(bf16[2,128,384]{2,1,0:T(8,128)(2,1)} %param.15) | copy-start | bytes 589828
  11.0 21.4 %copy-start.17 = (s32[16]{0:T(128)S(1)}, s32[16]{0:T(128)}, u32[]{:S(2)}) copy-start(s32[16]{0:T(128)} %param.20) | copy-start | bytes 196
  11.1 22.5 %copy-start.20 = (s32[16]{0:T(128)S(1)}, s32[16]{0:T(128)}, u32[]{:S(2)}) copy-start(s32[16]{0:T(128)} %param.22) | copy-start | bytes 196
  11.1 25.1 %copy-start.16 = (s32[16,4]{0,1:T(4,128)S(1)}, s32[16,4]{0,1:T(4,128)}, u32[]{:S(2)}) copy-start(s32[16,4]{0,1:T(4,128)} %param.21) | copy-start | bytes 772
  12.1 37.9 %collective-permute-start.9 = (bf16[2,512,384]{1,2,0:T(8,128)(2,1)}, bf16[2,512,384]{1,2,0:T(8,128)(2,1)}, u32[]{:S(2)}, u32[]{:S(2)}) collective-permute-start(bf16[2,512,384]{1,2,0:T(8,128)(2,1)} %pad_maximum_fusion), channel_id=1, source_target_pairs={{40,0},{48,8},{56,16},{64,24},{72,32},{80,40},{88,48},{96,56},{104... | collective-permute-start | bytes 2359304 | tf_op jit(solution)/shard_map/ppermute | solution.py:17
  13.4 107.8 %collective-permute-start.8 = (bf16[2,512,384]{1,2,0:T(8,128)(2,1)}, bf16[2,512,384]{1,2,0:T(8,128)(2,1)}, u32[]{:S(2)}, u32[]{:S(2)}) collective-permute-start(bf16[2,512,384]{1,2,0:T(8,128)(2,1)} %pad_maximum_fusion), channel_id=1, source_target_pairs={{0,40},{8,48},{16,56},{24,64},{32,72},{40,80},{48,88},{56,96},{64,... | collective-permute-start | bytes 2359304 | tf_op jit(solution)/shard_map/ppermute | solution.py:17
  23.9 99.7 %collective-permute-start.7 = (bf16[2,512,384]{1,2,0:T(8,128)(2,1)}, bf16[2,512,384]{1,2,0:T(8,128)(2,1)}, u32[]{:S(2)}, u32[]{:S(2)}) collective-permute-start(bf16[2,512,384]{1,2,0:T(8,128)(2,1)} %pad_maximum_fusion), channel_id=1, source_target_pairs={{32,0},{40,8},{48,16},{56,24},{64,32},{72,40},{80,48},{88,56},{96,... | collective-permute-start | bytes 2359304 | tf_op jit(solution)/shard_map/ppermute | solution.py:17
  25.2 112.8 %collective-permute-start.6 = (bf16[2,512,384]{1,2,0:T(8,128)(2,1)}, bf16[2,512,384]{1,2,0:T(8,128)(2,1)}, u32[]{:S(2)}, u32[]{:S(2)}) collective-permute-start(bf16[2,512,384]{1,2,0:T(8,128)(2,1)} %pad_maximum_fusion), channel_id=1, source_target_pairs={{0,32},{8,40},{16,48},{24,56},{32,64},{40,72},{48,80},{56,88},{64,... | collective-permute-start | bytes 2359304 | tf_op jit(solution)/shard_map/ppermute | solution.py:17
  31.0 151.9 %collective-permute-start.5 = (bf16[2,512,384]{1,2,0:T(8,128)(2,1)}, bf16[2,512,384]{1,2,0:T(8,128)(2,1)}, u32[]{:S(2)}, u32[]{:S(2)}) collective-permute-start(bf16[2,512,384]{1,2,0:T(8,128)(2,1)} %pad_maximum_fusion), channel_id=1, source_target_pairs={{24,0},{32,8},{40,16},{48,24},{56,32},{64,40},{72,48},{80,56},{88,... | collective-permute-start | bytes 2359304 | tf_op jit(solution)/shard_map/ppermute | solution.py:17
  40.8 3.6 copy-start.15
  40.8 3.6 copy-start.14
  41.8 4.0 copy-start.11
  50.0 157.7 %collective-permute-start.4 = (bf16[2,512,384]{1,2,0:T(8,128)(2,1)}, bf16[2,512,384]{1,2,0:T(8,128)(2,1)S(1)}, u32[]{:S(2)}, u32[]{:S(2)}) collective-permute-start(bf16[2,512,384]{1,2,0:T(8,128)(2,1)} %pad_maximum_fusion), channel_id=1, source_target_pairs={{0,24},{8,32},{16,40},{24,48},{32,56},{40,64},{48,72},{56,80},{64,... | collective-permute-start | bytes 2359304 | tf_op jit(solution)/shard_map/ppermute | solution.py:17
  121.2 121.9 %collective-permute-start.3 = (bf16[2,512,384]{1,2,0:T(8,128)(2,1)}, bf16[2,512,384]{1,2,0:T(8,128)(2,1)S(1)}, u32[]{:S(2)}, u32[]{:S(2)}) collective-permute-start(bf16[2,512,384]{1,2,0:T(8,128)(2,1)} %pad_maximum_fusion), channel_id=1, source_target_pairs={{16,0},{24,8},{32,16},{40,24},{48,32},{56,40},{64,48},{72,56},{80,... | collective-permute-start | bytes 2359304 | tf_op jit(solution)/shard_map/ppermute | solution.py:17
  123.7 121.9 %collective-permute-start.2 = (bf16[2,512,384]{1,2,0:T(8,128)(2,1)}, bf16[2,512,384]{1,2,0:T(8,128)(2,1)S(1)}, u32[]{:S(2)}, u32[]{:S(2)}) collective-permute-start(bf16[2,512,384]{1,2,0:T(8,128)(2,1)} %pad_maximum_fusion), channel_id=1, source_target_pairs={{0,16},{8,24},{16,32},{24,40},{32,48},{40,56},{48,64},{56,72},{64,... | collective-permute-start | bytes 2359304 | tf_op jit(solution)/shard_map/ppermute | solution.py:17
  138.0 108.6 %collective-permute-start.1 = (bf16[2,512,384]{1,2,0:T(8,128)(2,1)}, bf16[2,512,384]{1,2,0:T(8,128)(2,1)S(1)}, u32[]{:S(2)}, u32[]{:S(2)}) collective-permute-start(bf16[2,512,384]{1,2,0:T(8,128)(2,1)} %pad_maximum_fusion), channel_id=1, source_target_pairs={{8,0},{16,8},{24,16},{32,24},{40,32},{48,40},{56,48},{64,56},{72,6... | collective-permute-start | bytes 2359304 | tf_op jit(solution)/shard_map/ppermute | solution.py:17
  182.9 65.2 %collective-permute-start.10 = (bf16[2,512,384]{1,2,0:T(8,128)(2,1)}, bf16[2,512,384]{1,2,0:T(8,128)(2,1)S(1)}, u32[]{:S(2)}, u32[]{:S(2)}) collective-permute-start(bf16[2,512,384]{1,2,0:T(8,128)(2,1)} %pad_maximum_fusion), channel_id=1, source_target_pairs={{0,48},{8,56},{16,64},{24,72},{32,80},{40,88},{48,96},{56,104},{64... | collective-permute-start | bytes 2359304 | tf_op jit(solution)/shard_map/ppermute | solution.py:17
  207.7 60.9 %collective-permute-start = (bf16[2,512,384]{1,2,0:T(8,128)(2,1)}, bf16[2,512,384]{1,2,0:T(8,128)(2,1)S(1)}, u32[]{:S(2)}, u32[]{:S(2)}) collective-permute-start(bf16[2,512,384]{1,2,0:T(8,128)(2,1)} %pad_maximum_fusion), channel_id=1, source_target_pairs={{0,8},{8,16},{16,24},{24,32},{32,40},{40,48},{48,56},{56,64},{64,7... | collective-permute-start | bytes 2359304 | tf_op jit(solution)/shard_map/ppermute | solution.py:17
  243.1 26.6 %collective-permute-start.11 = (bf16[2,512,384]{1,2,0:T(8,128)(2,1)}, bf16[2,512,384]{1,2,0:T(8,128)(2,1)S(1)}, u32[]{:S(2)}, u32[]{:S(2)}) collective-permute-start(bf16[2,512,384]{1,2,0:T(8,128)(2,1)} %pad_maximum_fusion), channel_id=1, source_target_pairs={{48,0},{56,8},{64,16},{72,24},{80,32},{88,40},{96,48},{104,56},{11... | collective-permute-start | bytes 2359304 | tf_op jit(solution)/shard_map/ppermute | solution.py:17
  246.6 0.9 copy-start.1
  247.6 0.9 copy-start.3
  248.0 0.9 copy-start.4
  249.0 19.7 %copy-start.2 = (pred[256,512]{0,1:T(8,128)(4,1)S(1)}, pred[256,512]{0,1:T(8,128)(4,1)}, u32[]{:S(2)}) copy-start(pred[256,512]{0,1:T(8,128)(4,1)} %pad_add_fusion.11) | copy-start | bytes 393220
  249.5 19.7 %copy-start.5 = (pred[256,512]{0,1:T(8,128)(4,1)S(1)}, pred[256,512]{0,1:T(8,128)(4,1)}, u32[]{:S(2)}) copy-start(pred[256,512]{0,1:T(8,128)(4,1)} %pad_add_fusion.1) | copy-start | bytes 393220
  269.2 0.9 copy-start.7
  269.7 1.4 copy-start.6
  269.7 1.4 copy-start.12
  274.6 0.9 copy-start.10
  274.6 1.0 copy-start.13
  281.4 1.9 copy-start.18
  282.6 212.2 %all-gather.5.cloned.1.call-start = ((), (), s32[]{:S(2)}) async-start(), calls=%async_computation.1 | async-start | bytes 3993600 | tf_op jit(solution)/shard_map/all_gather | solution.py:134
  283.3 211.4 %copy-start.19 = (bf16[256,640]{1,0:T(8,128)(2,1)S(1)}, bf16[256,640]{1,0:T(8,128)(2,1)}, u32[]{:S(2)}) copy-start(bf16[256,640]{1,0:T(8,128)(2,1)} %param.17) | copy-start | bytes 983044
Sparse Core Ops, SparseCore 0:
  282.7 91.4 all-gather.2
  376.3 118.3 all-gather.4
where the time goes:
time: 507 us; the launch traced here: 506 us
  waiting for transfers between devices  304 us (60%)
  starting transfers between devices  134 us (26%)
  matrix products  21.3 us (4%)
  local copies, waits for them, and re-layouts  19.2 us (4%)
  between operations  14.4 us (3%)
  other arithmetic  13.3 us (3%)
    ppermute x12, starting transfers between devices, shifted(): return lax.ppermute(block, axis, route)  134 us
    all_gather x1, waiting for transfers between devices, local(): lax.all_gather(out_weight, 'seq', axis=0, tiled=True)  121 us
    ppermute x12, waiting for transfers between devices, shifted(): return lax.ppermute(block, axis, route)  93.1 us
    all_gather x1, waiting for transfers between devices, local(): attention = lax.all_gather(attention_local, 'tensor', axis=1, tiled=True)  89.4 us
  transfers between devices with their start and end apart: 14, of which 5 were waited for; matrix products, arithmetic and copies ran while one was open for 6% of the time, Pallas kernels for 0%

commit v1 on v0

--- a/solution.py
+++ b/solution.py
@@ -129,10 +129,14 @@
         jnp.transpose(result, (1, 0, 2)).reshape(row_count, tile_width).astype(jnp.bfloat16)
     )
     attention = lax.all_gather(attention_local, "tensor", axis=1, tiled=True)
+
+    def task_report(block_here, mesh_ax, pos_dim):
+        z = tuple((block_here for _ in range(lax.psum(1, mesh_ax))))
+        out_arr = jnp.stack(z)
+        return jnp.concatenate(lax.all_to_all(out_arr, mesh_ax, 0, 0), axis=pos_dim)
+
     projected = jnp.dot(
-        attention,
-        lax.all_gather(out_weight, "seq", axis=0, tiled=True),
-        preferred_element_type=jnp.float32,
+        attention, task_report(out_weight, "seq", 0), preferred_element_type=jnp.float32
     )
     clip_total = lengths.shape[0]
     step_onehot = (

time: 507 us -> 472 us (0.931)
  waiting for transfers between devices: 304 us -> 241 us
  starting transfers between devices: 134 us -> 159 us
    all_gather x1 -> x0, waiting for transfers between devices: 121 us -> none  [local(): lax.all_gather(out_weight, 'seq', axis=0, tiled=True)]
    ppermute x12, waiting for transfers between devices: 93.1 us -> 150 us  [shifted(): return lax.ppermute(block, axis, route)]
    all_to_all x0 -> x1, starting transfers between devices: none -> 14.2 us  [task_report(): return jnp.concatenate(lax.all_to_all(out_arr, mesh_ax, 0, 0), axis=pos_dim)]
    ppermute x12, starting transfers between devices: 134 us -> 145 us  [shifted(): return lax.ppermute(block, axis, route)]
  transfers between devices with their start and end apart: 14 -> 14, of which waited for: 5 -> 4; matrix products, arithmetic and copies ran while one was open for 6% -> 9% of each run, Pallas kernels for 0% -> 0%
where the time goes in v1:
time: 472 us; the launch traced here: 471 us
  waiting for transfers between devices  241 us (51%)
  starting transfers between devices  159 us (34%)
  matrix products  21.4 us (5%)
  local copies, waits for them, and re-layouts  21.3 us (5%)
  between operations  14.4 us (3%)
  other arithmetic  13.3 us (3%)
    ppermute x12, waiting for transfers between devices, shifted(): return lax.ppermute(block, axis, route)  150 us
    ppermute x12, starting transfers between devices, shifted(): return lax.ppermute(block, axis, route)  145 us
    all_gather x1, waiting for transfers between devices, local(): attention = lax.all_gather(attention_local, 'tensor', axis=1, tiled=True)  90.7 us
    all_to_all x1, starting transfers between devices, task_report(): return jnp.concatenate(lax.all_to_all(out_arr, mesh_ax, 0, 0), axis=pos_dim)  14.2 us
  transfers between devices with their start and end apart: 14, of which 4 were waited for; matrix products, arithmetic and copies ran while one was open for 9% of the time, Pallas kernels for 0%

profile of v1, /device:TPU:1, one launch (start us, length us, event | category | flops | bytes accessed | tf_op | source)
XLA Modules:
  0.0 470.7 jit_solution(18345485536869258591)
XLA Ops:
  6.5 1.2 copy.107
  7.8 1.1 copy.113
  8.8 1.1 copy.196
  10.0 1.1 copy.197
  11.1 1.0 pad_maximum_fusion
  12.1 1.3 collective-permute-start.9
  13.4 10.5 %collective-permute-start.8 = (bf16[2,512,384]{1,2,0:T(8,128)(2,1)}, bf16[2,512,384]{1,2,0:T(8,128)(2,1)}, u32[]{:S(2)}, u32[]{:S(2)}) collective-permute-start(bf16[2,512,384]{1,2,0:T(8,128)(2,1)} %pad_maximum_fusion), channel_id=1, source_target_pairs={{0,40},{8,48},{16,56},{24,64},{32,72},{40,80},{48,88},{56,96},{64,... | collective-permute-start | bytes 2359304 | tf_op jit(solution)/shard_map/ppermute | solution.py:17
  23.9 1.3 collective-permute-start.7
  25.2 5.8 %collective-permute-start.6 = (bf16[2,512,384]{1,2,0:T(8,128)(2,1)}, bf16[2,512,384]{1,2,0:T(8,128)(2,1)}, u32[]{:S(2)}, u32[]{:S(2)}) collective-permute-start(bf16[2,512,384]{1,2,0:T(8,128)(2,1)} %pad_maximum_fusion), channel_id=1, source_target_pairs={{0,32},{8,40},{16,48},{24,56},{32,64},{40,72},{48,80},{56,88},{64,... | collective-permute-start | bytes 2359304 | tf_op jit(solution)/shard_map/ppermute | solution.py:17
  31.0 1.3 collective-permute-start.5
  32.3 2.2 stack.11
  34.5 14.2 %all-to-all-start = ((bf16[64,48,640]{2,1,0:T(8,128)(2,1)}), bf16[64,48,640]{2,1,0:T(8,128)(2,1)}, u32[]{:S(2)}, u32[]{:S(2)}) async-start(bf16[64,48,640]{2,1,0:T(8,128)(2,1)} %stack.11), calls=%async_computation | async-start | bytes 7864320 | tf_op jit(solution)/shard_map/all_to_all | solution.py:136
  49.3 0.7 convert_reduce_fusion
  50.0 1.1 copy.111
  51.1 0.8 copy.109
  51.9 0.7 copy.110
  52.8 0.7 and_reduce_fusion
  53.6 0.6 compare_and_fusion.10
  54.6 0.6 pad_add_fusion.4
  55.2 0.7 pad_add_fusion.3
  55.9 0.7 pad_add_fusion.2
  56.6 0.6 broadcast_and_fusion.12
  57.2 0.9 compare_and_fusion.1
  58.2 2.7 fusion.175
  61.0 0.7 pad_add_fusion.11
  61.7 0.7 pad_add_fusion.1
  62.4 0.7 pad_add_fusion.12
  63.0 1.8 copy.114
  64.8 1.7 concatenate.64
  66.5 4.5 collective-permute-start.4
  71.0 1.2 fusion.153
  72.2 113.7 %collective-permute-done.8 = bf16[2,512,384]{1,2,0:T(8,128)(2,1)} collective-permute-done((bf16[2,512,384]{1,2,0:T(8,128)(2,1)}, bf16[2,512,384]{1,2,0:T(8,128)(2,1)}, u32[]{:S(2)}, u32[]{:S(2)}) %collective-permute-start.8) | collective-permute-done | bytes 786464 | tf_op jit(solution)/shard_map/ppermute | solution.py:17
  185.9 1.3 collective-permute-start.3
  187.2 1.2 fusion.154
  188.4 4.0 collective-permute-start.2
  192.5 1.2 fusion.155
  193.6 17.3 %collective-permute-done.6 = bf16[2,512,384]{1,2,0:T(8,128)(2,1)} collective-permute-done((bf16[2,512,384]{1,2,0:T(8,128)(2,1)}, bf16[2,512,384]{1,2,0:T(8,128)(2,1)}, u32[]{:S(2)}, u32[]{:S(2)}) %collective-permute-start.6) | collective-permute-done | bytes 786464 | tf_op jit(solution)/shard_map/ppermute | solution.py:17
  210.9 50.0 %collective-permute-start.1 = (bf16[2,512,384]{1,2,0:T(8,128)(2,1)}, bf16[2,512,384]{1,2,0:T(8,128)(2,1)S(1)}, u32[]{:S(2)}, u32[]{:S(2)}) collective-permute-start(bf16[2,512,384]{1,2,0:T(8,128)(2,1)} %pad_maximum_fusion), channel_id=1, source_target_pairs={{8,0},{16,8},{24,16},{32,24},{40,32},{48,40},{56,48},{64,56},{72,6... | collective-permute-start | bytes 2359304 | tf_op jit(solution)/shard_map/ppermute | solution.py:17
  260.9 1.2 fusion.156
  262.1 23.6 %collective-permute-start.10 = (bf16[2,512,384]{1,2,0:T(8,128)(2,1)}, bf16[2,512,384]{1,2,0:T(8,128)(2,1)S(1)}, u32[]{:S(2)}, u32[]{:S(2)}) collective-permute-start(bf16[2,512,384]{1,2,0:T(8,128)(2,1)} %pad_maximum_fusion), channel_id=1, source_target_pairs={{0,48},{8,56},{16,64},{24,72},{32,80},{40,88},{48,96},{56,104},{64... | collective-permute-start | bytes 2359304 | tf_op jit(solution)/shard_map/ppermute | solution.py:17
  285.7 1.2 fusion.157
  286.9 40.1 %collective-permute-start = (bf16[2,512,384]{1,2,0:T(8,128)(2,1)}, bf16[2,512,384]{1,2,0:T(8,128)(2,1)S(1)}, u32[]{:S(2)}, u32[]{:S(2)}) collective-permute-start(bf16[2,512,384]{1,2,0:T(8,128)(2,1)} %pad_maximum_fusion), channel_id=1, source_target_pairs={{0,8},{8,16},{16,24},{24,32},{32,40},{40,48},{48,56},{56,64},{64,7... | collective-permute-start | bytes 2359304 | tf_op jit(solution)/shard_map/ppermute | solution.py:17
  327.1 0.5 fusion.165
  327.6 1.5 collective-permute-start.11
  329.1 0.5 fusion.166
  329.6 0.5 fusion.167
  330.1 0.5 fusion.168
  330.6 0.5 fusion.169
  331.2 0.5 fusion.170
  332.0 0.5 fusion.171
  332.9 0.5 fusion.172
  333.4 0.5 fusion.173
  333.9 19.1 %collective-permute-done = bf16[2,512,384]{1,2,0:T(8,128)(2,1)S(1)} collective-permute-done((bf16[2,512,384]{1,2,0:T(8,128)(2,1)}, bf16[2,512,384]{1,2,0:T(8,128)(2,1)S(1)}, u32[]{:S(2)}, u32[]{:S(2)}) %collective-permute-start) | collective-permute-done | bytes 786464 | tf_op jit(solution)/shard_map/ppermute | solution.py:17
  353.1 0.5 fusion.164
  353.6 0.5 fusion.174
  354.5 0.5 fusion.163
  355.1 0.6 copy-done.6
  360.5 0.5 fusion.42
  362.8 0.7 fusion.47
  365.8 1.1 fusion.54
  367.0 0.9 fusion.113
  367.9 0.5 fusion.146
  368.4 90.7 %all-gather.2.cloned.1.call-done = bf16[256,3072]{0,1:T(8,128)(2,1)} async-done(((bf16[256,384]{0,1:T(8,128)(2,1)}), bf16[256,3072]{0,1:T(8,128)(2,1)}) %all-gather.2.cloned.1.call-update) | async-done | bytes 1572880 | tf_op jit(solution)/shard_map/all_gather | solution.py:131
  459.1 4.7 %fusion.27 = bf16[256,640]{1,0:T(8,128)(2,1)} fusion(f32[256,640]{1,0:T(8,128)S(1)} %fusion.146, bf16[256,3072]{0,1:T(8,128)(2,1)} %all-gather.2.cloned.1.call-done, bf16[3072,640]{1,0:T(8,128)(2,1)} %bitcast.98, bf16[256,640]{1,0:T(8,128)(2,1)S(1)} %copy-done.20), kind=kOutput, calls=%fused_computation.54 | convolution fusion | flops 1007288320 | bytes 6815744 | tf_op jit(solution)/shard_map/dot_general | solution.py:138
  (142 shorter events, 11.5 us)
Async XLA Ops:
  6.5 360.4 %copy-start = (f32[1000,640]{1,0:T(8,128)S(1)}, f32[1000,640]{1,0:T(8,128)}, u32[]{:S(2)}) copy-start(f32[1000,640]{1,0:T(8,128)} %param.19) | copy-start | bytes 7680004
  8.8 3.2 copy-start.9
  11.0 21.3 %copy-start.14 = (bf16[48,640]{1,0:T(8,128)(2,1)S(1)}, bf16[48,640]{1,0:T(8,128)(2,1)}, u32[]{:S(2)}) copy-start(bf16[48,640]{1,0:T(8,128)(2,1)} %param.18) | copy-start | bytes 184324
  12.1 54.5 %collective-permute-start.9 = (bf16[2,512,384]{1,2,0:T(8,128)(2,1)}, bf16[2,512,384]{1,2,0:T(8,128)(2,1)}, u32[]{:S(2)}, u32[]{:S(2)}) collective-permute-start(bf16[2,512,384]{1,2,0:T(8,128)(2,1)} %pad_maximum_fusion), channel_id=1, source_target_pairs={{40,0},{48,8},{56,16},{64,24},{72,32},{80,40},{88,48},{96,56},{104... | collective-permute-start | bytes 2359304 | tf_op jit(solution)/shard_map/ppermute | solution.py:17
  13.4 172.6 %collective-permute-start.8 = (bf16[2,512,384]{1,2,0:T(8,128)(2,1)}, bf16[2,512,384]{1,2,0:T(8,128)(2,1)}, u32[]{:S(2)}, u32[]{:S(2)}) collective-permute-start(bf16[2,512,384]{1,2,0:T(8,128)(2,1)} %pad_maximum_fusion), channel_id=1, source_target_pairs={{0,40},{8,48},{16,56},{24,64},{32,72},{40,80},{48,88},{56,96},{64,... | collective-permute-start | bytes 2359304 | tf_op jit(solution)/shard_map/ppermute | solution.py:17
  23.9 164.5 %collective-permute-start.7 = (bf16[2,512,384]{1,2,0:T(8,128)(2,1)}, bf16[2,512,384]{1,2,0:T(8,128)(2,1)}, u32[]{:S(2)}, u32[]{:S(2)}) collective-permute-start(bf16[2,512,384]{1,2,0:T(8,128)(2,1)} %pad_maximum_fusion), channel_id=1, source_target_pairs={{32,0},{40,8},{48,16},{56,24},{64,32},{72,40},{80,48},{88,56},{96,... | collective-permute-start | bytes 2359304 | tf_op jit(solution)/shard_map/ppermute | solution.py:17
  25.2 185.7 %collective-permute-start.6 = (bf16[2,512,384]{1,2,0:T(8,128)(2,1)}, bf16[2,512,384]{1,2,0:T(8,128)(2,1)}, u32[]{:S(2)}, u32[]{:S(2)}) collective-permute-start(bf16[2,512,384]{1,2,0:T(8,128)(2,1)} %pad_maximum_fusion), channel_id=1, source_target_pairs={{0,32},{8,40},{16,48},{24,56},{32,64},{40,72},{48,80},{56,88},{64,... | collective-permute-start | bytes 2359304 | tf_op jit(solution)/shard_map/ppermute | solution.py:17
  31.0 231.1 %collective-permute-start.5 = (bf16[2,512,384]{1,2,0:T(8,128)(2,1)}, bf16[2,512,384]{1,2,0:T(8,128)(2,1)}, u32[]{:S(2)}, u32[]{:S(2)}) collective-permute-start(bf16[2,512,384]{1,2,0:T(8,128)(2,1)} %pad_maximum_fusion), channel_id=1, source_target_pairs={{24,0},{32,8},{40,16},{48,24},{56,32},{64,40},{72,48},{80,56},{88,... | collective-permute-start | bytes 2359304 | tf_op jit(solution)/shard_map/ppermute | solution.py:17
  34.5 14.4 %copy-start.8 = (bf16[2,128,384]{2,1,0:T(8,128)(2,1)S(1)}, bf16[2,128,384]{2,1,0:T(8,128)(2,1)}, u32[]{:S(2)}) copy-start(bf16[2,128,384]{2,1,0:T(8,128)(2,1)} %param.15) | copy-start | bytes 589828
  34.5 14.5 %copy-start.18 = (s32[16]{0:T(128)S(1)}, s32[16]{0:T(128)}, u32[]{:S(2)}) copy-start(s32[16]{0:T(128)} %param.20) | copy-start | bytes 196
  34.5 15.5 %copy-start.21 = (s32[16]{0:T(128)S(1)}, s32[16]{0:T(128)}, u32[]{:S(2)}) copy-start(s32[16]{0:T(128)} %param.22) | copy-start | bytes 196
  34.5 424.6 %all-to-all-start = ((bf16[64,48,640]{2,1,0:T(8,128)(2,1)}), bf16[64,48,640]{2,1,0:T(8,128)(2,1)}, u32[]{:S(2)}, u32[]{:S(2)}) async-start(bf16[64,48,640]{2,1,0:T(8,128)(2,1)} %stack.11), calls=%async_computation | async-start | bytes 7864320 | tf_op jit(solution)/shard_map/all_to_all | solution.py:136
  48.7 4.0 copy-start.17
  48.7 410.4 %all-gather.2.cloned.1.call-start = ((), (), s32[]{:S(2)}) async-start(), calls=%async_computation.1 | async-start | bytes 1769472 | tf_op jit(solution)/shard_map/all_gather | solution.py:131
  57.2 3.7 copy-start.16
  57.2 3.7 copy-start.15
  58.2 4.1 copy-start.11
  66.5 220.4 %collective-permute-start.4 = (bf16[2,512,384]{1,2,0:T(8,128)(2,1)}, bf16[2,512,384]{1,2,0:T(8,128)(2,1)S(1)}, u32[]{:S(2)}, u32[]{:S(2)}) collective-permute-start(bf16[2,512,384]{1,2,0:T(8,128)(2,1)} %pad_maximum_fusion), channel_id=1, source_target_pairs={{0,24},{8,32},{16,40},{24,48},{32,56},{40,64},{48,72},{56,80},{64,... | collective-permute-start | bytes 2359304 | tf_op jit(solution)/shard_map/ppermute | solution.py:17
  185.9 141.6 %collective-permute-start.3 = (bf16[2,512,384]{1,2,0:T(8,128)(2,1)}, bf16[2,512,384]{1,2,0:T(8,128)(2,1)S(1)}, u32[]{:S(2)}, u32[]{:S(2)}) collective-permute-start(bf16[2,512,384]{1,2,0:T(8,128)(2,1)} %pad_maximum_fusion), channel_id=1, source_target_pairs={{16,0},{24,8},{32,16},{40,24},{48,32},{56,40},{64,48},{72,56},{80,... | collective-permute-start | bytes 2359304 | tf_op jit(solution)/shard_map/ppermute | solution.py:17
  188.4 141.7 %collective-permute-start.2 = (bf16[2,512,384]{1,2,0:T(8,128)(2,1)}, bf16[2,512,384]{1,2,0:T(8,128)(2,1)S(1)}, u32[]{:S(2)}, u32[]{:S(2)}) collective-permute-start(bf16[2,512,384]{1,2,0:T(8,128)(2,1)} %pad_maximum_fusion), channel_id=1, source_target_pairs={{0,16},{8,24},{16,32},{24,40},{32,48},{40,56},{48,64},{56,72},{64,... | collective-permute-start | bytes 2359304 | tf_op jit(solution)/shard_map/ppermute | solution.py:17
  210.9 120.2 %collective-permute-start.1 = (bf16[2,512,384]{1,2,0:T(8,128)(2,1)}, bf16[2,512,384]{1,2,0:T(8,128)(2,1)S(1)}, u32[]{:S(2)}, u32[]{:S(2)}) collective-permute-start(bf16[2,512,384]{1,2,0:T(8,128)(2,1)} %pad_maximum_fusion), channel_id=1, source_target_pairs={{8,0},{16,8},{24,16},{32,24},{40,32},{48,40},{56,48},{64,56},{72,6... | collective-permute-start | bytes 2359304 | tf_op jit(solution)/shard_map/ppermute | solution.py:17
  262.1 70.4 %collective-permute-start.10 = (bf16[2,512,384]{1,2,0:T(8,128)(2,1)}, bf16[2,512,384]{1,2,0:T(8,128)(2,1)S(1)}, u32[]{:S(2)}, u32[]{:S(2)}) collective-permute-start(bf16[2,512,384]{1,2,0:T(8,128)(2,1)} %pad_maximum_fusion), channel_id=1, source_target_pairs={{0,48},{8,56},{16,64},{24,72},{32,80},{40,88},{48,96},{56,104},{64... | collective-permute-start | bytes 2359304 | tf_op jit(solution)/shard_map/ppermute | solution.py:17
  286.9 66.2 %collective-permute-start = (bf16[2,512,384]{1,2,0:T(8,128)(2,1)}, bf16[2,512,384]{1,2,0:T(8,128)(2,1)S(1)}, u32[]{:S(2)}, u32[]{:S(2)}) collective-permute-start(bf16[2,512,384]{1,2,0:T(8,128)(2,1)} %pad_maximum_fusion), channel_id=1, source_target_pairs={{0,8},{8,16},{16,24},{24,32},{32,40},{40,48},{48,56},{56,64},{64,7... | collective-permute-start | bytes 2359304 | tf_op jit(solution)/shard_map/ppermute | solution.py:17
  327.6 26.6 %collective-permute-start.11 = (bf16[2,512,384]{1,2,0:T(8,128)(2,1)}, bf16[2,512,384]{1,2,0:T(8,128)(2,1)S(1)}, u32[]{:S(2)}, u32[]{:S(2)}) collective-permute-start(bf16[2,512,384]{1,2,0:T(8,128)(2,1)} %pad_maximum_fusion), channel_id=1, source_target_pairs={{48,0},{56,8},{64,16},{72,24},{80,32},{88,40},{96,48},{104,56},{11... | collective-permute-start | bytes 2359304 | tf_op jit(solution)/shard_map/ppermute | solution.py:17
  331.1 0.9 copy-start.1
  332.0 0.9 copy-start.3
  332.5 0.9 copy-start.4
  333.4 19.7 %copy-start.2 = (pred[256,512]{0,1:T(8,128)(4,1)S(1)}, pred[256,512]{0,1:T(8,128)(4,1)}, u32[]{:S(2)}) copy-start(pred[256,512]{0,1:T(8,128)(4,1)} %pad_add_fusion.11) | copy-start | bytes 393220
  333.9 19.7 %copy-start.5 = (pred[256,512]{0,1:T(8,128)(4,1)S(1)}, pred[256,512]{0,1:T(8,128)(4,1)}, u32[]{:S(2)}) copy-start(pred[256,512]{0,1:T(8,128)(4,1)} %pad_add_fusion.1) | copy-start | bytes 393220
  353.6 0.9 copy-start.7
  354.2 1.4 copy-start.6
  354.2 1.4 copy-start.12
  359.0 0.9 copy-start.10
  359.1 1.0 copy-start.13
  365.8 1.2 copy-start.19
  367.0 92.1 %copy-start.20 = (bf16[256,640]{1,0:T(8,128)(2,1)S(1)}, bf16[256,640]{1,0:T(8,128)(2,1)}, u32[]{:S(2)}) copy-start(bf16[256,640]{1,0:T(8,128)(2,1)} %param.17) | copy-start | bytes 983044
Sparse Core Ops, SparseCore 0:
  367.1 91.9 all-gather.1
